TPU v7x, 32 devices: a whole 2x2x4 slice. The times are simulated.
32 devices in a mesh: rows: 4 (over y, core), cols: 8 (over z, x).
Axes of the slice: x: 2, y: 2, z: 4, core: 2. Of those that a mesh axis runs over, the one named last changes fastest.
Arguments:
- prior: float32 [64, 512, 512], P('rows', 'cols'), may hold values from -6 to 6
- obs_cell: int32 [8, 128], replicated, may hold values from 0 to 32767, as said below
- obs_weight: float32 [8, 128, 8], replicated, may hold values from 0.1 to 1
- obs_value: float32 [8, 128], replicated, may hold values from -8 to 8
- obs_var: float32 [8, 128], replicated, may hold values from 0.25 to 4
- loc_mask: int32 [8, 32], replicated, may hold values from 0 to 1, as said below
- batch_order: int32 [8], replicated, may hold values from 0 to 7, each once
- kernel: float32 [8, 7, 7], replicated, may hold values from 0.005 to 0.04
- mixing: float32 [8, 8], replicated, may hold values from -2 to 2
Outputs:
- forecast: float32 [64, 512, 512], P('rows', 'cols')
Inputs may be any that keep to these rules, and one draw needn't show every extreme that they name: `obs_cell`: all 128 cells of one batch lie in one tile, rows r * 16 to (r + 1) * 16 - 1 and columns c * 64 to (c + 1) * 64 - 1, whose index is r * 8 + c. `loc_mask`: for each batch the tiles marked 1 form a rectangle of tiles that contains the tile of that batch's cells. `batch_order`: each batch appears once.
All inputs are finite; a program needn't handle non-finite values.
Results may differ from a plain program's by a relative error of at most 0.0003.
Values sent between devices are 32-bit elements; how exact they have to be, the bound alone decides.
No kernel may reach another device: no remote copies, remote signals or barrier semaphores. Data moves between devices by JAX's collectives and lax.ppermute only.
A program may use at most 128 MiB of HBM per device.

v0:
```python
import jax
import jax.numpy as jnp
from jax import lax
from jax.sharding import PartitionSpec as P

BATCHES = 8
KW = 7
HALFW = 48


def with_halo(shard, sides, width):
    for axis, dim in sides:
        size, length = (lax.axis_size(axis), shard.shape[dim])
        up = [(i, (i + 1) % size) for i in range(size - 1)]
        down = [(j, i) for i, j in up]
        last = lax.slice_in_dim(shard, length - width, length, axis=dim)
        initial = lax.slice_in_dim(shard, 0, width, axis=dim)
        before = lax.ppermute(last, axis, up)
        after = lax.ppermute(initial, axis, down)
        shard = jnp.concatenate([before, shard, after], axis=dim)
    return shard


def taper_weights(ratio):
    clamped = jnp.maximum(ratio, 1.0)
    inner_part = (((-0.25 * ratio + 0.5) * ratio + 0.625) * ratio - 5.0 / 3.0) * ratio * ratio + 1.0
    outer_part = (
        ((((ratio / 12.0 - 0.5) * ratio + 0.625) * ratio + 5.0 / 3.0) * ratio - 5.0) * ratio
        + 4.0
        - 2.0 / (3.0 * clamped)
    )
    return jnp.where(ratio <= 1.0, inner_part, jnp.where(ratio < 2.0, outer_part, 0.0))


def batch_gain(predicted, value_row, var_row):
    mean_pred = jnp.mean(predicted, axis=1)
    spread = predicted - mean_pred[:, None]
    variance = jnp.sum(spread * spread, axis=1) / (predicted.shape[1] - 1)
    denominator = variance + var_row
    shrink = 1.0 / (1.0 + jnp.sqrt(var_row / denominator))
    kalman_gain = ((value_row - mean_pred)[:, None] - shrink[:, None] * spread) / denominator[
        :, None
    ]
    return (spread, kalman_gain)


def refresh_block(block, first_row, first_col, cell_row, cell_col, spread, kalman_gain, active):
    rows_count, cols_count, channels = block.shape
    members = spread.shape[1]
    species = channels // members
    row_pos = (first_row + jnp.arange(rows_count, dtype=jnp.int32)).astype(jnp.float32)
    col_pos = (first_col + jnp.arange(cols_count, dtype=jnp.int32)).astype(jnp.float32)
    row_gap = row_pos[:, None, None] - cell_row.astype(jnp.float32)[None, None, :]
    col_gap = col_pos[None, :, None] - cell_col.astype(jnp.float32)[None, None, :]
    squared = row_gap * row_gap + col_gap * col_gap
    taper = taper_weights(jnp.sqrt(squared) / HALFW) * active
    taper = taper.reshape(rows_count * cols_count, cell_row.shape[0])
    members_view = block.reshape(rows_count * cols_count, species, members)
    covariance = jnp.einsum(
        "psm,im->psi", members_view, spread, precision=lax.Precision.HIGHEST
    ) / (members - 1)
    increment = jnp.einsum(
        "psi,im->psm", covariance * taper[:, None, :], kalman_gain, precision=lax.Precision.HIGHEST
    )
    return (members_view + increment).reshape(rows_count, cols_count, channels)


def refresh_tile(ensemble, row_start, col_start, cell_row, cell_col, spread, kalman_gain, active):
    pieces = refresh_block(
        ensemble, row_start + 0, col_start, cell_row, cell_col, spread, kalman_gain, active
    )
    return pieces


def local_prediction(ensemble, cell_row, cell_col, weights_rows, row_start, col_start):
    tile_height, tile_width, channels = ensemble.shape
    species = weights_rows.shape[1]
    members = channels // species
    local_row = cell_row - row_start
    local_col = cell_col - col_start
    inside = (
        (local_row >= 0) & (local_row < tile_height) & (local_col >= 0) & (local_col < tile_width)
    )
    flat_index = jnp.clip(local_row, 0, tile_height - 1) * tile_width + jnp.clip(
        local_col, 0, tile_width - 1
    )
    picked = ensemble.reshape(tile_height * tile_width, species, members)[flat_index]
    predicted = jnp.einsum("is,ism->im", weights_rows, picked, precision=lax.Precision.HIGHEST)
    return jnp.where(inside[:, None], predicted, 0.0)


def shards(prior, obs_cell, obs_weight, obs_value, obs_var, loc_mask, batch_order, kernel, mixing):
    tile_height, tile_width, channels = prior.shape
    species = kernel.shape[0]
    members = channels // species
    cols_count = lax.axis_size("cols")
    grid_width = tile_width * cols_count
    row_start = lax.axis_index("rows") * tile_height
    col_start = lax.axis_index("cols") * tile_width
    my_tile = lax.axis_index("rows") * cols_count + lax.axis_index("cols")
    ensemble = prior
    for position in range(BATCHES):
        current = batch_order[position]
        obs_cells = obs_cell[current]
        cell_row = obs_cells // grid_width
        cell_col = obs_cells % grid_width
        partial_value = local_prediction(
            ensemble, cell_row, cell_col, obs_weight[current], row_start, col_start
        )
        predicted = lax.psum(partial_value, ("rows", "cols"))
        spread, kalman_gain = batch_gain(predicted, obs_value[current], obs_var[current])
        active = loc_mask[current, my_tile].astype(jnp.float32)
        ensemble = refresh_tile(
            ensemble, row_start, col_start, cell_row, cell_col, spread, kalman_gain, active
        )
    halo_width = KW // 2
    padded = with_halo(ensemble, (("rows", 0), ("cols", 1)), 3)
    padded_width = tile_width + 2 * halo_width
    offsets = (
        jnp.arange(padded_width, dtype=jnp.int32)[None, :]
        - jnp.arange(tile_width, dtype=jnp.int32)[:, None]
    )
    onehot = (offsets[:, :, None] == jnp.arange(KW, dtype=jnp.int32)[None, None, :]).astype(
        jnp.float32
    )
    band_matrix = jnp.einsum("tak,xik->taxi", kernel, onehot, precision=lax.Precision.HIGHEST)
    padded_grid = padded.reshape(tile_height + 2 * halo_width, padded_width, species, members)
    smoothed = jnp.zeros((tile_height, tile_width, species, members), jnp.float32)
    for vertical in range(KW):
        smoothed = smoothed + jnp.einsum(
            "txi,yitm->yxtm",
            band_matrix[:, vertical],
            padded_grid[vertical : vertical + tile_height],
            precision=lax.Precision.HIGHEST,
        )
    mixed_field = jnp.einsum("st,yxtm->yxsm", mixing, smoothed, precision=lax.Precision.HIGHEST)
    return mixed_field.reshape(tile_height, tile_width, channels)


def solution(mesh):
    return jax.shard_map(
        shards,
        mesh=mesh,
        in_specs=(P("rows", "cols", None), P(), P(), P(), P(), P(), P(), P(), P()),
        out_specs=P("rows", "cols", None),
        check_vma=False,
    )
```

profile of v0, /device:TPU:1, one launch (start us, length us, event | category | flops | bytes accessed | tf_op | source)
XLA Modules:
  0.0 676.1 jit_solution(12245388337613379013)
XLA Ops:
  29.4 3.6 gather_fusion
  34.7 40.8 %psum.56 = f32[128,64]{0,1:T(8,128)S(1)} all-reduce(f32[128,64]{0,1:T(8,128)S(1)} %broadcast_select_fusion.7), channel_id=1, replica_groups=mesh['rows'=4,'cols'=8] {'rows','cols'}, use_global_device_ids=true, to_apply=%region_0.1 | all-reduce | flops 8192 | bytes 65536 | tf_op jit(solution)/shard_map/psum | solution.py:110
  80.4 4.5 fusion.60
  91.1 40.8 %psum.57 = f32[128,64]{0,1:T(8,128)S(1)} all-reduce(f32[128,64]{0,1:T(8,128)S(1)} %broadcast_select_fusion.6), channel_id=1, replica_groups=mesh['rows'=4,'cols'=8] {'rows','cols'}, use_global_device_ids=true, to_apply=%region_3.4 | all-reduce | flops 8192 | bytes 65536 | tf_op jit(solution)/shard_map/psum | solution.py:110
  131.9 6.8 %fusion.242 = f32[1024,8,128]{2,0,1:T(8,128)S(1)} fusion(f32[1024,8,64]{0,2,1:T(8,128)S(1)} %fusion.60, f32[128,64]{0,1:T(8,128)S(1)} %psum.57, f32[128]{0:T(128)S(1)} %get-tuple-element.169), kind=kOutput, calls=%fused_computation.329 | convolution fusion | flops 805314560 | bytes 6324736 | tf_op jit(solution)/shard_map/psm,im->psi/dot_general | solution.py:59
  140.1 6.3 fusion.39
  146.4 4.1 copy.69
  153.8 40.1 %psum.58 = f32[128,64]{0,1:T(8,128)S(1)} all-reduce(f32[128,64]{0,1:T(8,128)S(1)} %broadcast_select_fusion.5), channel_id=1, replica_groups=mesh['rows'=4,'cols'=8] {'rows','cols'}, use_global_device_ids=true, to_apply=%region_6.7 | all-reduce | flops 8192 | bytes 65536 | tf_op jit(solution)/shard_map/psum | solution.py:110
  194.1 6.8 %fusion.239 = f32[1024,8,128]{2,0,1:T(8,128)S(1)} fusion(f32[1024,8,64]{0,2,1:T(8,128)S(1)} %copy-done.2, f32[128,64]{0,1:T(8,128)S(1)} %psum.58, f32[128]{0:T(128)S(1)} %get-tuple-element.167), kind=kOutput, calls=%fused_computation.326 | convolution fusion | flops 805314560 | bytes 6324736 | tf_op jit(solution)/shard_map/psm,im->psi/dot_general | solution.py:59
  202.3 6.3 fusion.42
  208.6 4.4 copy.70
  216.3 40.2 %psum.59 = f32[128,64]{0,1:T(8,128)S(1)} all-reduce(f32[128,64]{0,1:T(8,128)S(1)} %broadcast_select_fusion.4), channel_id=1, replica_groups=mesh['rows'=4,'cols'=8] {'rows','cols'}, use_global_device_ids=true, to_apply=%region_9.10 | all-reduce | flops 8192 | bytes 65536 | tf_op jit(solution)/shard_map/psum | solution.py:110
  256.6 6.8 %fusion.236 = f32[1024,8,128]{2,0,1:T(8,128)S(1)} fusion(f32[1024,8,64]{0,2,1:T(8,128)S(1)} %copy-done.3, f32[128,64]{0,1:T(8,128)S(1)} %psum.59, f32[128]{0:T(128)S(1)} %get-tuple-element.165), kind=kOutput, calls=%fused_computation.323 | convolution fusion | flops 805314560 | bytes 6324736 | tf_op jit(solution)/shard_map/psm,im->psi/dot_general | solution.py:59
  264.8 6.3 fusion.45
  271.1 4.1 copy.71
  278.6 40.1 %psum.60 = f32[128,64]{0,1:T(8,128)S(1)} all-reduce(f32[128,64]{0,1:T(8,128)S(1)} %broadcast_select_fusion.3), channel_id=1, replica_groups=mesh['rows'=4,'cols'=8] {'rows','cols'}, use_global_device_ids=true, to_apply=%region_12.13 | all-reduce | flops 8192 | bytes 65536 | tf_op jit(solution)/shard_map/psum | solution.py:110
  318.8 6.8 %fusion.233 = f32[1024,8,128]{2,0,1:T(8,128)S(1)} fusion(f32[1024,8,64]{0,2,1:T(8,128)S(1)} %copy-done.4, f32[128,64]{0,1:T(8,128)S(1)} %psum.60, f32[128]{0:T(128)S(1)} %get-tuple-element.163), kind=kOutput, calls=%fused_computation.320 | convolution fusion | flops 805314560 | bytes 6324736 | tf_op jit(solution)/shard_map/psm,im->psi/dot_general | solution.py:59
  327.0 6.3 fusion.48
  333.3 4.4 copy.72
  341.0 40.2 %psum.61 = f32[128,64]{0,1:T(8,128)S(1)} all-reduce(f32[128,64]{0,1:T(8,128)S(1)} %broadcast_select_fusion.2), channel_id=1, replica_groups=mesh['rows'=4,'cols'=8] {'rows','cols'}, use_global_device_ids=true, to_apply=%region_15.16 | all-reduce | flops 8192 | bytes 65536 | tf_op jit(solution)/shard_map/psum | solution.py:110
  381.4 6.8 %fusion.230 = f32[1024,8,128]{2,0,1:T(8,128)S(1)} fusion(f32[1024,8,64]{0,2,1:T(8,128)S(1)} %copy-done.5, f32[128,64]{0,1:T(8,128)S(1)} %psum.61, f32[128]{0:T(128)S(1)} %get-tuple-element.161), kind=kOutput, calls=%fused_computation.317 | convolution fusion | flops 805314560 | bytes 6324736 | tf_op jit(solution)/shard_map/psm,im->psi/dot_general | solution.py:59
  389.6 6.3 fusion.51
  395.9 4.0 copy.73
  403.2 40.3 %psum.62 = f32[128,64]{0,1:T(8,128)S(1)} all-reduce(f32[128,64]{0,1:T(8,128)S(1)} %broadcast_select_fusion.1), channel_id=1, replica_groups=mesh['rows'=4,'cols'=8] {'rows','cols'}, use_global_device_ids=true, to_apply=%region_18.19 | all-reduce | flops 8192 | bytes 65536 | tf_op jit(solution)/shard_map/psum | solution.py:110
  443.5 6.8 %fusion.227 = f32[1024,8,128]{2,0,1:T(8,128)S(1)} fusion(f32[1024,8,64]{0,2,1:T(8,128)S(1)} %copy-done.6, f32[128,64]{0,1:T(8,128)S(1)} %psum.62, f32[128]{0:T(128)S(1)} %get-tuple-element.159), kind=kOutput, calls=%fused_computation.314 | convolution fusion | flops 805314560 | bytes 6324736 | tf_op jit(solution)/shard_map/psm,im->psi/dot_general | solution.py:59
  451.6 4.9 fusion.54
  462.7 40.7 %psum.63 = f32[128,64]{0,1:T(8,128)S(1)} all-reduce(f32[128,64]{0,1:T(8,128)S(1)} %broadcast_select_fusion), channel_id=1, replica_groups=mesh['rows'=4,'cols'=8] {'rows','cols'}, use_global_device_ids=true, to_apply=%region_21.22 | all-reduce | flops 8192 | bytes 65536 | tf_op jit(solution)/shard_map/psum | solution.py:110
  503.5 6.8 %fusion.224 = f32[1024,8,128]{2,0,1:T(8,128)S(1)} fusion(f32[1024,8,64]{0,2,1:T(8,128)S(1)} %fusion.54, f32[128,64]{0,1:T(8,128)S(1)} %psum.63, f32[128]{0:T(128)S(1)} %get-tuple-element.133), kind=kOutput, calls=%fused_computation.311 | convolution fusion | flops 805314560 | bytes 6324736 | tf_op jit(solution)/shard_map/psm,im->psi/dot_general | solution.py:59
  511.6 4.9 fusion.57
  521.4 5.4 collective-permute-start
  542.9 3.9 collective-permute-done.2
  548.4 5.2 fusion.409
  553.6 4.6 reshape.2901
  558.2 4.6 reshape.2900
  562.8 4.6 reshape.2905
  567.4 4.6 reshape.2904
  572.0 4.6 reshape.2903
  576.7 4.6 reshape.2902
  583.9 10.3 %fusion.10 = f32[8,16,64,64]{3,2,1,0:T(8,128)S(1)} fusion(f32[16,70,8,64]{3,2,1,0:T(8,128)} %reshape.2901, f32[8,64,70,1]{2,0,1,3:T(8,128)} %get-tuple-element.61), kind=kOutput, calls=%fused_computation.18 | convolution fusion | flops 440401920 | bytes 4534272 | tf_op jit(solution)/shard_map/txi,yitm->yxtm/dot_general | solution.py:130
  594.2 11.8 %fusion.12 = f32[8,16,64,64]{3,2,1,0:T(8,128)} fusion(f32[16,70,8,64]{3,2,1,0:T(8,128)} %reshape.2900, f32[8,64,70,1]{2,0,1,3:T(8,128)S(1)} %copy-done.17), kind=kOutput, calls=%fused_computation.20 | convolution fusion | flops 440401920 | bytes 4534272 | tf_op jit(solution)/shard_map/txi,yitm->yxtm/dot_general | solution.py:130
  606.1 9.4 %fusion.2 = f32[8,16,64,64]{3,2,1,0:T(8,128)} fusion(f32[16,70,8,64]{3,2,1,0:T(8,128)S(1)} %bitcast.856, f32[8,64,70,1]{2,0,1,3:T(8,128)S(1)} %copy-done.16), kind=kOutput, calls=%fused_computation.10 | convolution fusion | flops 440401920 | bytes 4534272 | tf_op jit(solution)/shard_map/txi,yitm->yxtm/dot_general | solution.py:130
  615.5 9.9 %fusion.4 = f32[8,16,64,64]{3,2,1,0:T(8,128)} fusion(f32[16,70,8,64]{3,2,1,0:T(8,128)S(1)} %bitcast.854, f32[8,64,70,1]{2,0,1,3:T(8,128)S(1)} %copy-done.15), kind=kOutput, calls=%fused_computation.12 | convolution fusion | flops 440401920 | bytes 4534272 | tf_op jit(solution)/shard_map/txi,yitm->yxtm/dot_general | solution.py:130
  625.4 9.5 %fusion.6 = f32[8,16,64,64]{3,2,1,0:T(8,128)} fusion(f32[16,70,8,64]{3,2,1,0:T(8,128)S(1)} %bitcast.852, f32[8,64,70,1]{2,0,1,3:T(8,128)S(1)} %copy-done.14), kind=kOutput, calls=%fused_computation.14 | convolution fusion | flops 440401920 | bytes 4534272 | tf_op jit(solution)/shard_map/txi,yitm->yxtm/dot_general | solution.py:130
  635.0 9.4 %fusion.8 = f32[8,16,64,64]{3,2,1,0:T(8,128)} fusion(f32[16,70,8,64]{3,2,1,0:T(8,128)S(1)} %bitcast.850, f32[8,64,70,1]{2,0,1,3:T(8,128)S(1)} %get-tuple-element.60), kind=kOutput, calls=%fused_computation.16 | convolution fusion | flops 440401920 | bytes 4534272 | tf_op jit(solution)/shard_map/txi,yitm->yxtm/dot_general | solution.py:130
  644.4 13.5 %add_bitcast_fusion = f32[16,64,8,64]{1,3,0,2:T(8,128)} fusion(f32[8,16,64,64]{3,2,1,0:T(8,128)S(1)} %copy-done.10, f32[8,16,64,64]{3,2,1,0:T(8,128)} %fusion.4, f32[8,16,64,64]{3,2,1,0:T(8,128)} %fusion.6, f32[8,16,64,64]{3,2,1,0:T(8,128)} %fusion.8, f32[8,16,64,64]{3,2,1,0:T(8,128)S(1)} %copy-done.9, f32[8,16,64,64]{3,2,1,0:T(8,128)S(1)} %fusion.10, ...), kind=kOutput, calls=%fused_computation.24 | convolution fusion | flops 443547648 | bytes 17117184 | tf_op jit(solution)/shard_map/txi,yitm->yxtm/dot_general | solution.py:130
  657.9 5.3 copy.99
  663.3 7.8 %convolution_bitcast_fusion = f32[16,64,8,64]{3,2,1,0:T(8,128)} fusion(f32[16,64,8,64]{3,2,1,0:T(8,128)} %copy.99, f32[8,8]{1,0:T(8,128)S(1)} %copy-done.45), kind=kOutput, calls=%fused_computation.40 | convolution fusion | flops 50331648 | bytes 4194560 | tf_op jit(solution)/shard_map/st,yxtm->yxsm/dot_general | solution.py:136
  671.1 4.8 reshape.2792
  (290 shorter events, 79.5 us)
Async XLA Ops:
  0.0 534.7 %copy-start = (f32[8,7,7]{2,0,1:T(8,128)S(1)}, f32[8,7,7]{2,0,1:T(8,128)}, u32[]{:S(2)}) copy-start(f32[8,7,7]{2,0,1:T(8,128)} %param.16) | copy-start | bytes 4708
  0.0 24.1 %copy-start.13 = (f32[16,64,512]{2,1,0:T(8,128)S(1)}, f32[16,64,512]{2,1,0:T(8,128)}, u32[]{:S(2)}) copy-start(f32[16,64,512]{2,1,0:T(8,128)} %param.9) | copy-start | bytes 6291460
  29.4 50.4 %copy-start.8 = (f32[1024,8,64]{0,2,1:T(8,128)}, f32[1024,8,64]{0,2,1:T(8,128)S(1)}, u32[]{:S(2)}) copy-start(f32[1024,8,64]{0,2,1:T(8,128)S(1)} %copy.67) | copy-start | bytes 6291460
  85.0 46.9 %copy-start.46 = (f32[8,128]{1,0:T(8,128)S(1)}, f32[8,128]{1,0:T(8,128)}, u32[]{:S(2)}) copy-start(f32[8,128]{1,0:T(8,128)} %param.12) | copy-start | bytes 12292
  87.7 51.0 %copy-start.47 = (f32[8,128]{1,0:T(8,128)S(1)}, f32[8,128]{1,0:T(8,128)}, u32[]{:S(2)}) copy-start(f32[8,128]{1,0:T(8,128)} %param.13) | copy-start | bytes 12292
  87.8 51.6 %copy-start.22 = (f32[16,128]{1,0:T(8,128)S(1)}, f32[16,128]{1,0:T(8,128)}, u32[]{:S(2)}) copy-start(f32[16,128]{1,0:T(8,128)} %get-tuple-element.135) | copy-start | bytes 24580
  146.3 7.4 %copy-start.41 = (s32[128]{0:T(128)S(1)}, s32[128]{0:T(128)}, u32[]{:S(2)}) copy-start(s32[128]{0:T(128)} %copy-done.40) | copy-start | bytes 1540
  146.3 7.5 %copy-start.53 = (s32[128]{0:T(128)S(1)}, s32[128]{0:T(128)}, u32[]{:S(2)}) copy-start(s32[128]{0:T(128)} %get-tuple-element.107) | copy-start | bytes 1540
  146.4 47.7 %copy-start.2 = (f32[1024,8,64]{0,2,1:T(8,128)S(1)}, f32[1024,8,64]{0,2,1:T(8,128)}, u32[]{:S(2)}) copy-start(f32[1024,8,64]{0,2,1:T(8,128)} %fusion.39) | copy-start | bytes 6291460
  150.5 51.0 %copy-start.21 = (f32[16,128]{1,0:T(8,128)S(1)}, f32[16,128]{1,0:T(8,128)}, u32[]{:S(2)}) copy-start(f32[16,128]{1,0:T(8,128)} %get-tuple-element.136) | copy-start | bytes 24580
  208.6 7.7 %copy-start.39 = (s32[128]{0:T(128)S(1)}, s32[128]{0:T(128)}, u32[]{:S(2)}) copy-start(s32[128]{0:T(128)} %copy-done.38) | copy-start | bytes 1540
  208.6 7.7 %copy-start.52 = (s32[128]{0:T(128)S(1)}, s32[128]{0:T(128)}, u32[]{:S(2)}) copy-start(s32[128]{0:T(128)} %get-tuple-element.104) | copy-start | bytes 1540
  208.6 48.0 %copy-start.3 = (f32[1024,8,64]{0,2,1:T(8,128)S(1)}, f32[1024,8,64]{0,2,1:T(8,128)}, u32[]{:S(2)}) copy-start(f32[1024,8,64]{0,2,1:T(8,128)} %fusion.42) | copy-start | bytes 6291460
  213.0 51.1 %copy-start.20 = (f32[16,128]{1,0:T(8,128)S(1)}, f32[16,128]{1,0:T(8,128)}, u32[]{:S(2)}) copy-start(f32[16,128]{1,0:T(8,128)} %get-tuple-element.137) | copy-start | bytes 24580
  271.1 7.4 %copy-start.37 = (s32[128]{0:T(128)S(1)}, s32[128]{0:T(128)}, u32[]{:S(2)}) copy-start(s32[128]{0:T(128)} %copy-done.36) | copy-start | bytes 1540
  271.1 7.5 %copy-start.51 = (s32[128]{0:T(128)S(1)}, s32[128]{0:T(128)}, u32[]{:S(2)}) copy-start(s32[128]{0:T(128)} %get-tuple-element.122) | copy-start | bytes 1540
  271.1 47.7 %copy-start.4 = (f32[1024,8,64]{0,2,1:T(8,128)S(1)}, f32[1024,8,64]{0,2,1:T(8,128)}, u32[]{:S(2)}) copy-start(f32[1024,8,64]{0,2,1:T(8,128)} %fusion.45) | copy-start | bytes 6291460
  275.3 51.0 %copy-start.19 = (f32[16,128]{1,0:T(8,128)S(1)}, f32[16,128]{1,0:T(8,128)}, u32[]{:S(2)}) copy-start(f32[16,128]{1,0:T(8,128)} %get-tuple-element.138) | copy-start | bytes 24580
  333.3 7.7 %copy-start.35 = (s32[128]{0:T(128)S(1)}, s32[128]{0:T(128)}, u32[]{:S(2)}) copy-start(s32[128]{0:T(128)} %copy-done.34) | copy-start | bytes 1540
  333.3 7.7 %copy-start.50 = (s32[128]{0:T(128)S(1)}, s32[128]{0:T(128)}, u32[]{:S(2)}) copy-start(s32[128]{0:T(128)} %get-tuple-element.119) | copy-start | bytes 1540
  333.3 48.0 %copy-start.5 = (f32[1024,8,64]{0,2,1:T(8,128)S(1)}, f32[1024,8,64]{0,2,1:T(8,128)}, u32[]{:S(2)}) copy-start(f32[1024,8,64]{0,2,1:T(8,128)} %fusion.48) | copy-start | bytes 6291460
  337.7 51.1 %copy-start.18 = (f32[16,128]{1,0:T(8,128)S(1)}, f32[16,128]{1,0:T(8,128)}, u32[]{:S(2)}) copy-start(f32[16,128]{1,0:T(8,128)} %get-tuple-element.139) | copy-start | bytes 24580
  395.8 7.3 %copy-start.33 = (s32[128]{0:T(128)S(1)}, s32[128]{0:T(128)}, u32[]{:S(2)}) copy-start(s32[128]{0:T(128)} %copy-done.32) | copy-start | bytes 1540
  395.8 7.3 %copy-start.49 = (s32[128]{0:T(128)S(1)}, s32[128]{0:T(128)}, u32[]{:S(2)}) copy-start(s32[128]{0:T(128)} %get-tuple-element.116) | copy-start | bytes 1540
  395.8 47.6 %copy-start.6 = (f32[1024,8,64]{0,2,1:T(8,128)S(1)}, f32[1024,8,64]{0,2,1:T(8,128)}, u32[]{:S(2)}) copy-start(f32[1024,8,64]{0,2,1:T(8,128)} %fusion.51) | copy-start | bytes 6291460
  443.5 8.1 %copy-start.7 = (f32[1024,8,64]{0,2,1:T(8,128)S(1)}, f32[1024,8,64]{0,2,1:T(8,128)}, u32[]{:S(2)}) copy-start(f32[1024,8,64]{0,2,1:T(8,128)} %fusion.51) | copy-start | bytes 6291460
  518.9 10.3 %copy-start.12 = (f32[1024,8,64]{0,2,1:T(8,128)S(1)}, f32[1024,8,64]{0,2,1:T(8,128)}, u32[]{:S(2)}) copy-start(f32[1024,8,64]{0,2,1:T(8,128)} %copy-done.11) | copy-start | bytes 6291460
  521.4 14.1 %collective-permute-start = (f32[3,64,512]{2,1,0:T(8,128)}, f32[3,64,512]{2,1,0:T(8,128)}, u32[]{:S(2)}, u32[]{:S(2)}) collective-permute-start(f32[3,64,512]{2,1,0:T(8,128)} %slice.114), channel_id=1, source_target_pairs={{0,8},{8,16},{16,24},{1,9},{9,17},{17,25},{2,10},{10,18},{18,26},{... | collective-permute-start | bytes 1179656 | tf_op jit(solution)/shard_map/ppermute | solution.py:18
  527.4 9.1 %collective-permute-start.1 = (f32[3,64,512]{2,1,0:T(8,128)S(1)}, f32[3,64,512]{2,1,0:T(8,128)S(1)}, u32[]{:S(2)}, u32[]{:S(2)}) collective-permute-start(f32[3,64,512]{2,1,0:T(8,128)S(1)} %slice.116), channel_id=1, source_target_pairs={{8,0},{16,8},{24,16},{9,1},{17,9},{25,17},{10,2},{18,10},{26,18},{... | collective-permute-start | bytes 1179656 | tf_op jit(solution)/shard_map/ppermute | solution.py:19
  537.4 9.4 %collective-permute-start.2 = (f32[22,3,512]{2,1,0:T(4,128)S(1)}, f32[22,3,512]{2,1,0:T(4,128)S(1)}, u32[]{:S(2)}, u32[]{:S(2)}) collective-permute-start(f32[22,3,512]{2,1,0:T(4,128)S(1)} %get-tuple-element.52), channel_id=1, source_target_pairs={{0,1},{1,2},{2,3},{3,4},{4,5},{5,6},{6,7},{8,9},{9,10},{10,11},{11... | collective-permute-start | bytes 405512 | tf_op jit(solution)/shard_map/ppermute | solution.py:18
  540.5 6.4 collective-permute-start.3
  581.3 24.8 %slice-start.6 = ((s8[4587520]{0:T(1024)(128)(4,1)}), s8[393216]{0:T(1024)(128)(4,1)S(1)}, s32[]{:S(2)}) async-start(s8[4587520]{0:T(1024)(128)(4,1)} %bitcast.855), calls=%async_computation.6 | async-start | bytes 786432
  583.9 10.3 %copy-start.17 = (f32[8,64,70,1]{2,0,1,3:T(8,128)S(1)}, f32[8,64,70,1]{2,0,1,3:T(8,128)}, u32[]{:S(2)}) copy-start(f32[8,64,70,1]{2,0,1,3:T(8,128)} %get-tuple-element.62) | copy-start | bytes 430084
  583.9 22.2 %slice-start.7 = ((s8[4587520]{0:T(1024)(128)(4,1)}), s8[4194304]{0:T(1024)(128)(4,1)S(1)}, s32[]{:S(2)}) async-start(s8[4587520]{0:T(1024)(128)(4,1)} %bitcast.855), calls=%async_computation.7 | async-start | bytes 8388608
  594.2 11.8 %copy-start.16 = (f32[8,64,70,1]{2,0,1,3:T(8,128)S(1)}, f32[8,64,70,1]{2,0,1,3:T(8,128)}, u32[]{:S(2)}) copy-start(f32[8,64,70,1]{2,0,1,3:T(8,128)} %get-tuple-element.57) | copy-start | bytes 430084
  594.2 21.3 %slice-start.4 = ((s8[4587520]{0:T(1024)(128)(4,1)}), s8[4194304]{0:T(1024)(128)(4,1)S(1)}, s32[]{:S(2)}) async-start(s8[4587520]{0:T(1024)(128)(4,1)} %bitcast.853), calls=%async_computation.4 | async-start | bytes 8388608
  594.2 31.2 %slice-start.2 = ((s8[4587520]{0:T(1024)(128)(4,1)}), s8[4194304]{0:T(1024)(128)(4,1)S(1)}, s32[]{:S(2)}) async-start(s8[4587520]{0:T(1024)(128)(4,1)} %bitcast.851), calls=%async_computation.2 | async-start | bytes 8388608
  606.1 9.4 %slice-start.5 = ((s8[4587520]{0:T(1024)(128)(4,1)}), s8[393216]{0:T(1024)(128)(4,1)S(1)}, s32[]{:S(2)}) async-start(s8[4587520]{0:T(1024)(128)(4,1)} %bitcast.853), calls=%async_computation.5 | async-start | bytes 786432
  606.1 9.4 %copy-start.15 = (f32[8,64,70,1]{2,0,1,3:T(8,128)S(1)}, f32[8,64,70,1]{2,0,1,3:T(8,128)}, u32[]{:S(2)}) copy-start(f32[8,64,70,1]{2,0,1,3:T(8,128)} %get-tuple-element.58) | copy-start | bytes 430084
  606.1 19.3 %slice-start.3 = ((s8[4587520]{0:T(1024)(128)(4,1)}), s8[393216]{0:T(1024)(128)(4,1)S(1)}, s32[]{:S(2)}) async-start(s8[4587520]{0:T(1024)(128)(4,1)} %bitcast.851), calls=%async_computation.3 | async-start | bytes 786432
  615.5 9.9 %copy-start.14 = (f32[8,64,70,1]{2,0,1,3:T(8,128)S(1)}, f32[8,64,70,1]{2,0,1,3:T(8,128)}, u32[]{:S(2)}) copy-start(f32[8,64,70,1]{2,0,1,3:T(8,128)} %get-tuple-element.59) | copy-start | bytes 430084
  615.5 19.4 %slice-start = ((s8[4587520]{0:T(1024)(128)(4,1)}), s8[4194304]{0:T(1024)(128)(4,1)S(1)}, s32[]{:S(2)}) async-start(s8[4587520]{0:T(1024)(128)(4,1)} %bitcast.849), calls=%async_computation | async-start | bytes 8388608
  625.4 9.6 %slice-start.1 = ((s8[4587520]{0:T(1024)(128)(4,1)}), s8[393216]{0:T(1024)(128)(4,1)S(1)}, s32[]{:S(2)}) async-start(s8[4587520]{0:T(1024)(128)(4,1)} %bitcast.849), calls=%async_computation.1 | async-start | bytes 786432
  625.4 19.0 %slice-start.8 = ((s8[4587520]{0:T(1024)(128)(4,1)}), s8[4194304]{0:T(1024)(128)(4,1)S(1)}, s32[]{:S(2)}) async-start(s8[4587520]{0:T(1024)(128)(4,1)} %bitcast.857), calls=%async_computation.8 | async-start | bytes 8388608
  635.0 9.4 %slice-start.9 = ((s8[4587520]{0:T(1024)(128)(4,1)}), s8[393216]{0:T(1024)(128)(4,1)S(1)}, s32[]{:S(2)}) async-start(s8[4587520]{0:T(1024)(128)(4,1)} %bitcast.857), calls=%async_computation.9 | async-start | bytes 786432
  635.0 9.4 %copy-start.9 = (f32[8,16,64,64]{3,2,1,0:T(8,128)S(1)}, f32[8,16,64,64]{3,2,1,0:T(8,128)}, u32[]{:S(2)}) copy-start(f32[8,16,64,64]{3,2,1,0:T(8,128)} %fusion.12) | copy-start | bytes 6291460
  635.0 9.4 %copy-start.10 = (f32[8,16,64,64]{3,2,1,0:T(8,128)S(1)}, f32[8,16,64,64]{3,2,1,0:T(8,128)}, u32[]{:S(2)}) copy-start(f32[8,16,64,64]{3,2,1,0:T(8,128)} %fusion.2) | copy-start | bytes 6291460
  663.3 12.6 %copy-start.1 = (f32[8,7,7]{2,0,1:T(8,128)S(1)}, f32[8,7,7]{2,0,1:T(8,128)}, u32[]{:S(2)}) copy-start(f32[8,7,7]{2,0,1:T(8,128)} %param.16) | copy-start | bytes 4708
  (28 other events, 120.7 us)
where the time goes:
time: 687 us; the launch traced here: 676 us
  blocking collectives  323 us (47%)
  matrix products  179 us (26%)
  local copies, waits for them, and re-layouts  118 us (17%)
  between operations  21.8 us (3%)
  other arithmetic  17 us (2%)
  starting transfers between devices  11.7 us (2%)
    psum x8, blocking collectives, shards(): predicted = lax.psum(partial_value, ('rows', 'cols'))  323 us
    dot_general x7, matrix products, shards(): jnp.einsum('txi,yitm->yxtm', band_matrix[:, vertical], padded_grid[vertic...  73.8 us
    dot_general x8, matrix products, refresh_block(): jnp.einsum('psm,im->psi', members_view, spread, precision=lax.Precision.H...  50.9 us
    dot_general x8, matrix products, refresh_block(): jnp.einsum('psi,im->psm', covariance * taper[:, None, :], kalman_gain, pr...  45.7 us
    slice x8, local copies, waits for them, and re-layouts, shards(): padded_grid[vertical:vertical + tile_height]  35.5 us
    add x7, local copies, waits for them, and re-layouts, refresh_block(): return (members_view + increment).reshape(rows_count, cols_count, channels)  26.4 us
    gather x8, local copies, waits for them, and re-layouts, local_prediction(): ensemble.reshape(tile_height * tile_width, species, members)[flat_index]  23.4 us
  transfers between devices with their start and end apart: 4, of which 3 were waited for; matrix products, arithmetic and copies ran while one was open for 1% of the time, Pallas kernels for 0%

commit v1 on v0

--- a/solution.py
+++ b/solution.py
@@ -107,7 +107,8 @@
         partial_value = local_prediction(
             ensemble, cell_row, cell_col, obs_weight[current], row_start, col_start
         )
-        predicted = lax.psum(partial_value, ("rows", "cols"))
+        step_on_lines = lambda buf: lax.all_gather(buf, ("rows", "cols")).sum(axis=0)
+        predicted = step_on_lines(partial_value)
         spread, kalman_gain = batch_gain(predicted, obs_value[current], obs_var[current])
         active = loc_mask[current, my_tile].astype(jnp.float32)
         ensemble = refresh_tile(

time: 687 us -> 802 us (1.17)
  waiting for transfers between devices: 4.9 us -> 411 us
  blocking collectives: 323 us -> 0 us
  between operations: 21.8 us -> 34.8 us
  other arithmetic: 17 us -> 28 us
    all_gather x0 -> x8, waiting for transfers between devices: none -> 405 us  [shards(): lax.all_gather(buf, ('rows', 'cols')).sum(axis=0)]
    psum x8 -> x0, blocking collectives: 323 us -> none  [shards(): predicted = lax.psum(partial_value, ('rows', 'cols'))]
    unnamed x152 -> x96, local copies, waits for them, and re-layouts: 2.52 us -> 13.6 us
    reduce_sum x8 -> x16, other arithmetic: 0.2 us -> 10.5 us  [batch_gain(): mean_pred = jnp.mean(predicted, axis=1)]
  transfers between devices with their start and end apart: 4 -> 12, of which waited for: 3 -> 10; matrix products, arithmetic and copies ran while one was open for 1% -> 2% of each run, Pallas kernels for 0% -> 0%
where the time goes in v1:
time: 802 us; the launch traced here: 792 us
  waiting for transfers between devices  411 us (51%)
  matrix products  179 us (22%)
  local copies, waits for them, and re-layouts  126 us (16%)
  between operations  34.8 us (4%)
  other arithmetic  28 us (3%)
  starting transfers between devices  11.6 us (1%)
    all_gather x8, waiting for transfers between devices, shards(): lax.all_gather(buf, ('rows', 'cols')).sum(axis=0)  405 us
    dot_general x7, matrix products, shards(): jnp.einsum('txi,yitm->yxtm', band_matrix[:, vertical], padded_grid[vertic...  73.7 us
    dot_general x8, matrix products, refresh_block(): jnp.einsum('psm,im->psi', members_view, spread, precision=lax.Precision.H...  50.9 us
    dot_general x8, matrix products, refresh_block(): jnp.einsum('psi,im->psm', covariance * taper[:, None, :], kalman_gain, pr...  45 us
    slice x8, local copies, waits for them, and re-layouts, shards(): padded_grid[vertical:vertical + tile_height]  35.4 us
    add x7, local copies, waits for them, and re-layouts, refresh_block(): return (members_view + increment).reshape(rows_count, cols_count, channels)  23.8 us
    gather x8, local copies, waits for them, and re-layouts, local_prediction(): ensemble.reshape(tile_height * tile_width, species, members)[flat_index]  22.6 us
  transfers between devices with their start and end apart: 12, of which 10 were waited for; matrix products, arithmetic and copies ran while one was open for 2% of the time, Pallas kernels for 0%

profile of v1, /device:TPU:1, one launch (start us, length us, event | category | flops | bytes accessed | tf_op | source)
XLA Modules:
  0.0 791.5 jit_solution(15654982182627190231)
XLA Ops:
  18.1 4.4 reshape.2790
  37.9 49.4 %all-gather.17.cloned.1.call-done = f32[4096,64]{0,1:T(8,128)} async-done(((f32[128,64]{0,1:T(8,128)}), f32[4096,64]{0,1:T(8,128)}) %all-gather.17.cloned.1.call-update) | async-done | bytes 1048592 | tf_op jit(solution)/shard_map/all_gather | solution.py:110
  90.2 3.5 fusion.245
  93.8 4.5 fusion.60
  106.7 50.6 %all-gather.19.cloned.1.call-done = f32[4096,64]{0,1:T(8,128)} async-done(((f32[128,64]{0,1:T(8,128)}), f32[4096,64]{0,1:T(8,128)}) %all-gather.19.cloned.1.call-update) | async-done | bytes 1048592 | tf_op jit(solution)/shard_map/all_gather | solution.py:110
  160.2 6.8 fusion.242
  167.1 6.3 fusion.39
  173.4 3.8 copy.107
  182.7 50.8 %all-gather.21.cloned.1.call-done = f32[4096,64]{0,1:T(8,128)} async-done(((f32[128,64]{0,1:T(8,128)}), f32[4096,64]{0,1:T(8,128)}) %all-gather.21.cloned.1.call-update) | async-done | bytes 1048592 | tf_op jit(solution)/shard_map/all_gather | solution.py:110
  236.5 6.8 fusion.239
  243.3 5.0 fusion.42
  256.8 50.6 %all-gather.23.cloned.1.call-done = f32[4096,64]{0,1:T(8,128)} async-done(((f32[128,64]{0,1:T(8,128)}), f32[4096,64]{0,1:T(8,128)}) %all-gather.23.cloned.1.call-update) | async-done | bytes 1048592 | tf_op jit(solution)/shard_map/all_gather | solution.py:110
  310.3 6.8 fusion.236
  317.1 6.3 fusion.45
  323.4 3.8 copy.111
  332.8 50.8 %all-gather.25.cloned.1.call-done = f32[4096,64]{0,1:T(8,128)} async-done(((f32[128,64]{0,1:T(8,128)}), f32[4096,64]{0,1:T(8,128)}) %all-gather.25.cloned.1.call-update) | async-done | bytes 1048592 | tf_op jit(solution)/shard_map/all_gather | solution.py:110
  386.5 6.8 fusion.233
  393.3 5.0 fusion.48
  406.8 50.6 %all-gather.27.cloned.1.call-done = f32[4096,64]{0,1:T(8,128)} async-done(((f32[128,64]{0,1:T(8,128)}), f32[4096,64]{0,1:T(8,128)}) %all-gather.27.cloned.1.call-update) | async-done | bytes 1048592 | tf_op jit(solution)/shard_map/all_gather | solution.py:110
  460.3 6.8 fusion.230
  467.1 6.3 fusion.51
  473.5 3.8 copy.115
  482.8 50.8 %all-gather.29.cloned.1.call-done = f32[4096,64]{0,1:T(8,128)} async-done(((f32[128,64]{0,1:T(8,128)}), f32[4096,64]{0,1:T(8,128)}) %all-gather.29.cloned.1.call-update) | async-done | bytes 1048592 | tf_op jit(solution)/shard_map/all_gather | solution.py:110
  536.5 6.8 fusion.227
  543.3 6.3 fusion.54
  549.7 4.2 copy.117
  559.0 51.2 %all-gather.31.cloned.1.call-done = f32[4096,64]{0,1:T(8,128)} async-done(((f32[128,64]{0,1:T(8,128)}), f32[4096,64]{0,1:T(8,128)}) %all-gather.31.cloned.1.call-update) | async-done | bytes 1048592 | tf_op jit(solution)/shard_map/all_gather | solution.py:110
  613.1 6.8 fusion.224
  620.0 5.2 fusion.57
  629.9 3.1 collective-permute-start
  651.3 4.4 collective-permute-done.3
  657.2 5.2 fusion.409
  662.3 4.6 reshape.2917
  666.9 4.6 reshape.2916
  671.5 4.6 reshape.2921
  676.1 4.6 reshape.2920
  680.7 4.7 reshape.2919
  685.4 4.6 reshape.2918
  692.6 10.3 %fusion.10 = f32[8,16,64,64]{3,2,1,0:T(8,128)S(1)} fusion(f32[16,70,8,64]{3,2,1,0:T(8,128)} %reshape.2917, f32[8,64,70,1]{2,0,1,3:T(8,128)} %get-tuple-element.61), kind=kOutput, calls=%fused_computation.18 | convolution fusion | flops 440401920 | bytes 4534272 | tf_op jit(solution)/shard_map/txi,yitm->yxtm/dot_general | solution.py:131
  702.9 11.8 %fusion.12 = f32[8,16,64,64]{3,2,1,0:T(8,128)} fusion(f32[16,70,8,64]{3,2,1,0:T(8,128)} %reshape.2916, f32[8,64,70,1]{2,0,1,3:T(8,128)S(1)} %copy-done.17), kind=kOutput, calls=%fused_computation.20 | convolution fusion | flops 440401920 | bytes 4534272 | tf_op jit(solution)/shard_map/txi,yitm->yxtm/dot_general | solution.py:131
  714.8 9.4 %fusion.2 = f32[8,16,64,64]{3,2,1,0:T(8,128)} fusion(f32[16,70,8,64]{3,2,1,0:T(8,128)S(1)} %bitcast.912, f32[8,64,70,1]{2,0,1,3:T(8,128)S(1)} %copy-done.16), kind=kOutput, calls=%fused_computation.10 | convolution fusion | flops 440401920 | bytes 4534272 | tf_op jit(solution)/shard_map/txi,yitm->yxtm/dot_general | solution.py:131
  724.2 9.9 %fusion.4 = f32[8,16,64,64]{3,2,1,0:T(8,128)} fusion(f32[16,70,8,64]{3,2,1,0:T(8,128)S(1)} %bitcast.910, f32[8,64,70,1]{2,0,1,3:T(8,128)S(1)} %copy-done.15), kind=kOutput, calls=%fused_computation.12 | convolution fusion | flops 440401920 | bytes 4534272 | tf_op jit(solution)/shard_map/txi,yitm->yxtm/dot_general | solution.py:131
  734.1 9.5 %fusion.6 = f32[8,16,64,64]{3,2,1,0:T(8,128)} fusion(f32[16,70,8,64]{3,2,1,0:T(8,128)S(1)} %bitcast.908, f32[8,64,70,1]{2,0,1,3:T(8,128)S(1)} %copy-done.14), kind=kOutput, calls=%fused_computation.14 | convolution fusion | flops 440401920 | bytes 4534272 | tf_op jit(solution)/shard_map/txi,yitm->yxtm/dot_general | solution.py:131
  743.7 9.4 %fusion.8 = f32[8,16,64,64]{3,2,1,0:T(8,128)} fusion(f32[16,70,8,64]{3,2,1,0:T(8,128)S(1)} %bitcast.906, f32[8,64,70,1]{2,0,1,3:T(8,128)S(1)} %get-tuple-element.60), kind=kOutput, calls=%fused_computation.16 | convolution fusion | flops 440401920 | bytes 4534272 | tf_op jit(solution)/shard_map/txi,yitm->yxtm/dot_general | solution.py:131
  753.1 13.5 %add_bitcast_fusion = f32[16,64,8,64]{1,3,0,2:T(8,128)} fusion(f32[8,16,64,64]{3,2,1,0:T(8,128)S(1)} %copy-done.10, f32[8,16,64,64]{3,2,1,0:T(8,128)} %fusion.4, f32[8,16,64,64]{3,2,1,0:T(8,128)} %fusion.6, f32[8,16,64,64]{3,2,1,0:T(8,128)} %fusion.8, f32[8,16,64,64]{3,2,1,0:T(8,128)S(1)} %copy-done.9, f32[8,16,64,64]{3,2,1,0:T(8,128)S(1)} %fusion.10, ...), kind=kOutput, calls=%fused_computation.24 | convolution fusion | flops 443547648 | bytes 17117184 | tf_op jit(solution)/shard_map/txi,yitm->yxtm/dot_general | solution.py:131
  766.6 5.4 copy.143
  771.9 7.8 convolution_bitcast_fusion
  779.7 4.8 reshape.2792
  (262 shorter events, 103.9 us)
Async XLA Ops:
  6.5 629.0 %copy-start = (f32[8,7,7]{2,0,1:T(8,128)S(1)}, f32[8,7,7]{2,0,1:T(8,128)}, u32[]{:S(2)}) copy-start(f32[8,7,7]{2,0,1:T(8,128)} %param.16) | copy-start | bytes 4708
  6.5 20.9 %copy-start.19 = (s32[8,128]{1,0:T(8,128)S(1)}, s32[8,128]{1,0:T(8,128)}, u32[]{:S(2)}) copy-start(s32[8,128]{1,0:T(8,128)} %param.10) | copy-start | bytes 12292
  6.5 21.0 %copy-start.18 = (f32[8,128,8]{1,2,0:T(8,128)S(1)}, f32[8,128,8]{1,2,0:T(8,128)}, u32[]{:S(2)}) copy-start(f32[8,128,8]{1,2,0:T(8,128)} %param.11) | copy-start | bytes 98308
  6.5 80.8 %all-gather.17.cloned.1.call-start = ((), (), s32[]{:S(2)}) async-start(), calls=%async_computation | async-start | bytes 1081344 | tf_op jit(solution)/shard_map/all_gather | solution.py:110
  27.6 7.6 copy-start.21
  32.2 125.2 %all-gather.19.cloned.1.call-start = ((), (), s32[]{:S(2)}) async-start(), calls=%async_computation.1 | async-start | bytes 1081344 | tf_op jit(solution)/shard_map/all_gather | solution.py:110
  35.1 55.1 %copy-start.8 = (f32[1024,8,64]{0,2,1:T(8,128)}, f32[1024,8,64]{0,2,1:T(8,128)S(1)}, u32[]{:S(2)}) copy-start(f32[1024,8,64]{0,2,1:T(8,128)S(1)} %copy.104) | copy-start | bytes 6291460
  36.8 53.3 %copy-start.22 = (f32[8,128]{1,0:T(8,128)S(1)}, f32[8,128]{1,0:T(8,128)}, u32[]{:S(2)}) copy-start(f32[8,128]{1,0:T(8,128)} %param.12) | copy-start | bytes 12292
  98.2 7.7 copy-start.28
  98.2 7.7 copy-start.29
  104.8 128.8 %all-gather.21.cloned.1.call-start = ((), (), s32[]{:S(2)}) async-start(), calls=%async_computation.2 | async-start | bytes 1081344 | tf_op jit(solution)/shard_map/all_gather | solution.py:110
  180.3 56.2 %copy-start.3 = (f32[1024,8,64]{0,2,1:T(8,128)S(1)}, f32[1024,8,64]{0,2,1:T(8,128)}, u32[]{:S(2)}) copy-start(f32[1024,8,64]{0,2,1:T(8,128)} %fusion.39) | copy-start | bytes 6291460
  181.0 126.4 %all-gather.23.cloned.1.call-start = ((), (), s32[]{:S(2)}) async-start(), calls=%async_computation.3 | async-start | bytes 1081344 | tf_op jit(solution)/shard_map/all_gather | solution.py:110
  236.4 6.9 copy-start.4
  248.3 7.8 copy-start.26
  248.3 7.8 copy-start.27
  254.8 128.8 %all-gather.25.cloned.1.call-start = ((), (), s32[]{:S(2)}) async-start(), calls=%async_computation.4 | async-start | bytes 1081344 | tf_op jit(solution)/shard_map/all_gather | solution.py:110
  330.3 56.2 %copy-start.5 = (f32[1024,8,64]{0,2,1:T(8,128)S(1)}, f32[1024,8,64]{0,2,1:T(8,128)}, u32[]{:S(2)}) copy-start(f32[1024,8,64]{0,2,1:T(8,128)} %fusion.45) | copy-start | bytes 6291460
  331.0 126.4 %all-gather.27.cloned.1.call-start = ((), (), s32[]{:S(2)}) async-start(), calls=%async_computation.5 | async-start | bytes 1081344 | tf_op jit(solution)/shard_map/all_gather | solution.py:110
  386.4 6.9 copy-start.6
  398.3 7.7 copy-start.24
  398.3 7.7 copy-start.25
  404.9 128.8 %all-gather.29.cloned.1.call-start = ((), (), s32[]{:S(2)}) async-start(), calls=%async_computation.6 | async-start | bytes 1081344 | tf_op jit(solution)/shard_map/all_gather | solution.py:110
  480.3 56.2 %copy-start.2 = (f32[1024,8,64]{0,2,1:T(8,128)S(1)}, f32[1024,8,64]{0,2,1:T(8,128)}, u32[]{:S(2)}) copy-start(f32[1024,8,64]{0,2,1:T(8,128)} %fusion.51) | copy-start | bytes 6291460
  481.1 129.2 %all-gather.31.cloned.1.call-start = ((), (), s32[]{:S(2)}) async-start(), calls=%async_computation.7 | async-start | bytes 1081344 | tf_op jit(solution)/shard_map/all_gather | solution.py:110
  557.0 56.2 %copy-start.7 = (f32[1024,8,64]{0,2,1:T(8,128)S(1)}, f32[1024,8,64]{0,2,1:T(8,128)}, u32[]{:S(2)}) copy-start(f32[1024,8,64]{0,2,1:T(8,128)} %fusion.54) | copy-start | bytes 6291460
  627.4 10.3 %copy-start.12 = (f32[1024,8,64]{0,2,1:T(8,128)S(1)}, f32[1024,8,64]{0,2,1:T(8,128)}, u32[]{:S(2)}) copy-start(f32[1024,8,64]{0,2,1:T(8,128)} %copy-done.11) | copy-start | bytes 6291460
  629.9 13.1 %collective-permute-start = (f32[3,64,512]{2,1,0:T(8,128)}, f32[3,64,512]{2,1,0:T(8,128)}, u32[]{:S(2)}, u32[]{:S(2)}) collective-permute-start(f32[3,64,512]{2,1,0:T(8,128)} %slice.114), channel_id=1, source_target_pairs={{0,8},{8,16},{16,24},{1,9},{9,17},{17,25},{2,10},{10,18},{18,26},{... | collective-permute-start | bytes 1179656 | tf_op jit(solution)/shard_map/ppermute | solution.py:18
  633.6 9.4 %collective-permute-start.1 = (f32[3,64,512]{2,1,0:T(8,128)S(1)}, f32[3,64,512]{2,1,0:T(8,128)S(1)}, u32[]{:S(2)}, u32[]{:S(2)}) collective-permute-start(f32[3,64,512]{2,1,0:T(8,128)S(1)} %slice.116), channel_id=1, source_target_pairs={{8,0},{16,8},{24,16},{9,1},{17,9},{25,17},{10,2},{18,10},{26,18},{... | collective-permute-start | bytes 1179656 | tf_op jit(solution)/shard_map/ppermute | solution.py:19
  644.1 7.2 collective-permute-start.2
  647.2 8.4 %collective-permute-start.3 = (f32[22,3,512]{2,1,0:T(4,128)S(1)}, f32[22,3,512]{2,1,0:T(4,128)S(1)}, u32[]{:S(2)}, u32[]{:S(2)}) collective-permute-start(f32[22,3,512]{2,1,0:T(4,128)S(1)} %get-tuple-element.53), channel_id=1, source_target_pairs={{1,0},{2,1},{3,2},{4,3},{5,4},{6,5},{7,6},{9,8},{10,9},{11,10},{12... | collective-permute-start | bytes 405512 | tf_op jit(solution)/shard_map/ppermute | solution.py:19
  690.0 24.8 %slice-start.6 = ((s8[4587520]{0:T(1024)(128)(4,1)}), s8[393216]{0:T(1024)(128)(4,1)S(1)}, s32[]{:S(2)}) async-start(s8[4587520]{0:T(1024)(128)(4,1)} %bitcast.911), calls=%async_computation.14 | async-start | bytes 786432
  692.6 10.3 %copy-start.17 = (f32[8,64,70,1]{2,0,1,3:T(8,128)S(1)}, f32[8,64,70,1]{2,0,1,3:T(8,128)}, u32[]{:S(2)}) copy-start(f32[8,64,70,1]{2,0,1,3:T(8,128)} %get-tuple-element.62) | copy-start | bytes 430084
  692.6 22.2 %slice-start.7 = ((s8[4587520]{0:T(1024)(128)(4,1)}), s8[4194304]{0:T(1024)(128)(4,1)S(1)}, s32[]{:S(2)}) async-start(s8[4587520]{0:T(1024)(128)(4,1)} %bitcast.911), calls=%async_computation.15 | async-start | bytes 8388608
  702.9 11.9 %copy-start.16 = (f32[8,64,70,1]{2,0,1,3:T(8,128)S(1)}, f32[8,64,70,1]{2,0,1,3:T(8,128)}, u32[]{:S(2)}) copy-start(f32[8,64,70,1]{2,0,1,3:T(8,128)} %get-tuple-element.57) | copy-start | bytes 430084
  702.9 21.3 %slice-start.4 = ((s8[4587520]{0:T(1024)(128)(4,1)}), s8[4194304]{0:T(1024)(128)(4,1)S(1)}, s32[]{:S(2)}) async-start(s8[4587520]{0:T(1024)(128)(4,1)} %bitcast.909), calls=%async_computation.12 | async-start | bytes 8388608
  702.9 31.2 %slice-start.2 = ((s8[4587520]{0:T(1024)(128)(4,1)}), s8[4194304]{0:T(1024)(128)(4,1)S(1)}, s32[]{:S(2)}) async-start(s8[4587520]{0:T(1024)(128)(4,1)} %bitcast.907), calls=%async_computation.10 | async-start | bytes 8388608
  714.8 9.4 %slice-start.5 = ((s8[4587520]{0:T(1024)(128)(4,1)}), s8[393216]{0:T(1024)(128)(4,1)S(1)}, s32[]{:S(2)}) async-start(s8[4587520]{0:T(1024)(128)(4,1)} %bitcast.909), calls=%async_computation.13 | async-start | bytes 786432
  714.8 9.4 %copy-start.15 = (f32[8,64,70,1]{2,0,1,3:T(8,128)S(1)}, f32[8,64,70,1]{2,0,1,3:T(8,128)}, u32[]{:S(2)}) copy-start(f32[8,64,70,1]{2,0,1,3:T(8,128)} %get-tuple-element.58) | copy-start | bytes 430084
  714.8 19.3 %slice-start.3 = ((s8[4587520]{0:T(1024)(128)(4,1)}), s8[393216]{0:T(1024)(128)(4,1)S(1)}, s32[]{:S(2)}) async-start(s8[4587520]{0:T(1024)(128)(4,1)} %bitcast.907), calls=%async_computation.11 | async-start | bytes 786432
  724.2 9.9 %copy-start.14 = (f32[8,64,70,1]{2,0,1,3:T(8,128)S(1)}, f32[8,64,70,1]{2,0,1,3:T(8,128)}, u32[]{:S(2)}) copy-start(f32[8,64,70,1]{2,0,1,3:T(8,128)} %get-tuple-element.59) | copy-start | bytes 430084
  724.2 19.4 %slice-start = ((s8[4587520]{0:T(1024)(128)(4,1)}), s8[4194304]{0:T(1024)(128)(4,1)S(1)}, s32[]{:S(2)}) async-start(s8[4587520]{0:T(1024)(128)(4,1)} %bitcast.905), calls=%async_computation.8 | async-start | bytes 8388608
  734.1 9.5 %slice-start.1 = ((s8[4587520]{0:T(1024)(128)(4,1)}), s8[393216]{0:T(1024)(128)(4,1)S(1)}, s32[]{:S(2)}) async-start(s8[4587520]{0:T(1024)(128)(4,1)} %bitcast.905), calls=%async_computation.9 | async-start | bytes 786432
  734.1 18.9 %slice-start.8 = ((s8[4587520]{0:T(1024)(128)(4,1)}), s8[4194304]{0:T(1024)(128)(4,1)S(1)}, s32[]{:S(2)}) async-start(s8[4587520]{0:T(1024)(128)(4,1)} %bitcast.913), calls=%async_computation.16 | async-start | bytes 8388608
  743.6 9.4 %slice-start.9 = ((s8[4587520]{0:T(1024)(128)(4,1)}), s8[393216]{0:T(1024)(128)(4,1)S(1)}, s32[]{:S(2)}) async-start(s8[4587520]{0:T(1024)(128)(4,1)} %bitcast.913), calls=%async_computation.17 | async-start | bytes 786432
  743.6 9.4 %copy-start.9 = (f32[8,16,64,64]{3,2,1,0:T(8,128)S(1)}, f32[8,16,64,64]{3,2,1,0:T(8,128)}, u32[]{:S(2)}) copy-start(f32[8,16,64,64]{3,2,1,0:T(8,128)} %fusion.12) | copy-start | bytes 6291460
  743.7 9.4 %copy-start.10 = (f32[8,16,64,64]{3,2,1,0:T(8,128)S(1)}, f32[8,16,64,64]{3,2,1,0:T(8,128)}, u32[]{:S(2)}) copy-start(f32[8,16,64,64]{3,2,1,0:T(8,128)} %fusion.2) | copy-start | bytes 6291460
  771.9 12.5 %copy-start.1 = (f32[8,7,7]{2,0,1:T(8,128)S(1)}, f32[8,7,7]{2,0,1:T(8,128)}, u32[]{:S(2)}) copy-start(f32[8,7,7]{2,0,1:T(8,128)} %param.16) | copy-start | bytes 4708
  (4 other events, 17.2 us)
Sparse Core Ops, SparseCore 0:
  32.3 54.9 all-gather.16
  104.9 52.3 all-gather.18
  181.1 52.3 all-gather.20
  255.0 52.3 all-gather.22
  331.2 52.4 all-gather.24
  405.0 52.3 all-gather.26
  481.2 52.4 all-gather.28
  557.8 52.4 all-gather.30
